TPU v7x, 32 devices: a whole 2x2x4 slice. The times are simulated.
32 devices in a mesh: dp: 4 (over y, x), seq: 8 (over z, core).
Axes of the slice: x: 2, y: 2, z: 4, core: 2. Of those that a mesh axis runs over, the one named last changes fastest.
Arguments:
- layer_in: float32 [4096, 2048], P(('dp', 'seq')), may hold values from -6 to 6
- norm1_gain: float32 [2048], replicated, may hold values from 0.25 to 1.75
- qkv_weight: bfloat16 [2048, 6144], P('dp'), may hold values from -0.79549513 to 0.79549513
- out_weight: bfloat16 [2048, 2048], P('dp'), may hold values from -2 to 2
- norm2_gain: float32 [2048], replicated, may hold values from 0.25 to 1.75
- gate_up_weight: bfloat16 [2048, 16384], P('dp'), may hold values from -0.125 to 0.125
- down_weight: bfloat16 [2048, 8192], P('dp'), may hold values from -0.0625 to 0.0625
- cotangent: float32 [4096, 2048], P(('dp', 'seq')), may hold values from -6 to 6
Outputs:
- layer_out: float32 [4096, 2048], P(('dp', 'seq'))
- input_grad: float32 [4096, 2048], P(('dp', 'seq'))
- norm1_grad: float32 [2048], P(('dp', 'seq'))
- qkv_grad: float32 [2048, 6144], P(('dp', 'seq'))
- out_grad: float32 [2048, 2048], P(('dp', 'seq'))
- norm2_grad: float32 [2048], P(('dp', 'seq'))
- gate_up_grad: float32 [2048, 16384], P(('dp', 'seq'))
- down_grad: float32 [2048, 8192], P(('dp', 'seq'))
All inputs are finite; a program needn't handle non-finite values.
Results may differ from a plain program's by a relative error of at most 0.018.
Values may be sent and summed in bfloat16 or wider, within the bound.
No kernel may reach another device: no remote copies, remote signals or barrier semaphores. Data moves between devices by JAX's collectives and lax.ppermute only.
A program may use at most 384 MiB of HBM per device.

v0:
```python
import jax
import jax.numpy as jnp
from jax import lax
from jax.sharding import PartitionSpec as P

HD = 64
EPS = 1e-05
THETA = 130000.0


def rotary_tables(length, head_dim):
    half_dim = head_dim // 2
    inverse = THETA ** (-(jnp.arange(half_dim).astype(jnp.float32) * 2.0) / head_dim)
    angles = jnp.arange(length).astype(jnp.float32)[:, None] * inverse[None, :]
    cosine = jnp.cos(angles)
    sine = jnp.sin(angles)
    return (jnp.concatenate([cosine, cosine], 1), jnp.concatenate([sine, sine], 1))


def rotate(values, cosine, sine):
    half_dim = values.shape[-1] // 2
    turned = jnp.concatenate([-values[..., half_dim:], values[..., :half_dim]], -1)
    return values * cosine[:, None, :] + turned * sine[:, None, :]


def scores_for(queries, key_rot, first_row, length, score_scale):
    block_rows = queries.shape[0]
    raw_scores = (
        jnp.einsum("qhd,khd->hqk", queries, key_rot, preferred_element_type=jnp.float32)
        * score_scale
    )
    query_pos = first_row + jnp.arange(block_rows)
    key_pos = jnp.arange(length)
    allowed = key_pos[None, :] <= query_pos[:, None]
    return jnp.where(allowed[None], raw_scores, -1e30)


def attend_forward(query_rot, key_rot, value_heads):
    length, head_count, head_dim = query_rot.shape
    block_rows = min(512, length)
    score_scale = head_dim ** (-0.5)

    def one_block(block_index):
        first_row = block_index * block_rows
        queries = lax.dynamic_slice_in_dim(query_rot, first_row, block_rows, 0)
        scores = scores_for(queries, key_rot, first_row, length, score_scale)
        row_max = jnp.max(scores, axis=2, keepdims=True)
        row_total = jnp.sum(jnp.exp(scores - row_max), axis=2, keepdims=True)
        log_total = row_max + jnp.log(row_total)
        prob_low = jnp.exp(scores - log_total).astype(jnp.bfloat16)
        mixed = jnp.einsum(
            "hqk,khd->qhd", prob_low, value_heads, preferred_element_type=jnp.float32
        )
        return (mixed.astype(jnp.bfloat16), log_total[:, :, 0])

    mixed, log_total = lax.map(one_block, jnp.arange(length // block_rows))
    return (mixed.reshape(length, head_count, head_dim), log_total)


def attend_backward(query_rot, key_rot, value_heads, mixed, log_total, grad_mixed):
    length, head_count, head_dim = query_rot.shape
    block_rows = min(512, length)
    score_scale = head_dim ** (-0.5)
    row_delta = jnp.sum(grad_mixed.astype(jnp.float32) * mixed.astype(jnp.float32), axis=2)

    def one_block(carry, block_index):
        grad_keys, grad_values = carry
        first_row = block_index * block_rows
        queries = lax.dynamic_slice_in_dim(query_rot, first_row, block_rows, 0)
        grad_rows = lax.dynamic_slice_in_dim(grad_mixed, first_row, block_rows, 0)
        delta_rows = lax.dynamic_slice_in_dim(row_delta, first_row, block_rows, 0)
        scores = scores_for(queries, key_rot, first_row, length, score_scale)
        probs = jnp.exp(scores - log_total[block_index][:, :, None])
        prob_low = probs.astype(jnp.bfloat16)
        grad_values = grad_values + jnp.einsum(
            "hqk,qhd->khd", prob_low, grad_rows, preferred_element_type=jnp.float32
        )
        grad_probs = jnp.einsum(
            "qhd,khd->hqk", grad_rows, value_heads, preferred_element_type=jnp.float32
        )
        grad_scores = (score_scale * probs * (grad_probs - delta_rows.T[:, :, None])).astype(
            jnp.bfloat16
        )
        grad_queries = jnp.einsum(
            "hqk,khd->qhd", grad_scores, key_rot, preferred_element_type=jnp.float32
        )
        grad_keys = grad_keys + jnp.einsum(
            "hqk,qhd->khd", grad_scores, queries, preferred_element_type=jnp.float32
        )
        return ((grad_keys, grad_values), grad_queries)

    empty = jnp.zeros((length, head_count, head_dim), jnp.float32)
    (grad_keys, grad_values), grad_queries = lax.scan(
        one_block, (empty, empty), jnp.arange(length // block_rows)
    )
    return (grad_queries.reshape(length, head_count, head_dim), grad_keys, grad_values)


def norm_backward(grad_normed, normed, gain, inv_rms):
    grad_hat = grad_normed * gain
    return inv_rms * (grad_hat - normed * jnp.mean(grad_hat * normed, axis=1, keepdims=True))


def keep_step(source, weight_piece):
    running = jnp.dot(source, weight_piece, preferred_element_type=jnp.float32)
    return (running, weight_piece)


def keep_columns(source, weight_piece):
    partial_out = jnp.einsum("tf,rf->tr", source, weight_piece, preferred_element_type=jnp.float32)
    return (partial_out, weight_piece)


def row_product(left, right):
    return jnp.einsum("tr,tc->rc", left, right, preferred_element_type=jnp.float32)


def heads_from_tokens(token_block):
    gathered = lax.all_to_all(token_block, "seq", split_axis=2, concat_axis=0, tiled=True)
    return gathered.reshape(gathered.shape[0], gathered.shape[1], gathered.shape[3] // HD, HD)


def tokens_from_heads(head_block):
    row_total = head_block.shape[0]
    flattened = head_block.reshape(row_total, head_block.shape[1], 1, head_block.shape[2] * HD)
    return lax.all_to_all(flattened, "seq", split_axis=0, concat_axis=2, tiled=True)


def seq_major(rows_side, dp_count, group_count, shard_rows):
    token_rows = rows_side.shape[0]
    reordered = rows_side.reshape(token_rows, dp_count, group_count, shard_rows).transpose(
        0, 2, 1, 3
    )
    return reordered.reshape(token_rows, dp_count * group_count * shard_rows)


def shards(
    layer_in, norm1_gain, qkv_weight, out_weight, norm2_gain, gate_up_weight, down_weight, cotangent
):
    token_rows, model_width = layer_in.shape
    group_count = lax.axis_size("seq")
    dp_count = lax.axis_size("dp")
    group_width = model_width // group_count
    hidden_units = down_weight.shape[1]
    length = token_rows * group_count
    shard_rows = model_width // (dp_count * group_count)
    inv_rms1 = lax.rsqrt(jnp.mean(layer_in * layer_in, axis=1, keepdims=True) + EPS)
    normed1 = layer_in * inv_rms1
    xn_first = (normed1 * norm1_gain).astype(jnp.bfloat16)
    qkv_sum, qkv_full = keep_step(xn_first, lax.all_gather(qkv_weight, "dp", axis=0, tiled=True))
    qkv_low = qkv_sum.astype(jnp.bfloat16).reshape(token_rows, 3, group_count, group_width)
    head_qkv = heads_from_tokens(qkv_low)
    cosine, sine = rotary_tables(length, HD)
    query_rot = rotate(head_qkv[:, 0].astype(jnp.float32), cosine, sine).astype(jnp.bfloat16)
    key_rot = rotate(head_qkv[:, 1].astype(jnp.float32), cosine, sine).astype(jnp.bfloat16)
    value_heads = head_qkv[:, 2]
    mixed, log_total = attend_forward(query_rot, key_rot, value_heads)
    local_heads = mixed.shape[1]
    token_mixed = tokens_from_heads(mixed.reshape(length, 1, local_heads, HD))
    attn_low = token_mixed.reshape(token_rows, model_width)
    attn_sum, out_full = keep_step(attn_low, lax.all_gather(out_weight, "dp", axis=0, tiled=True))
    hidden_res = layer_in + attn_sum
    inv_rms2 = lax.rsqrt(jnp.mean(hidden_res * hidden_res, axis=1, keepdims=True) + EPS)
    normed2 = hidden_res * inv_rms2
    xn_second = (normed2 * norm2_gain).astype(jnp.bfloat16)
    gate_up, gate_up_full = keep_step(
        xn_second, lax.all_gather(gate_up_weight, "dp", axis=0, tiled=True)
    )
    gate = gate_up[:, :hidden_units]
    up_part = gate_up[:, hidden_units:]
    sigmoid_gate = jax.nn.sigmoid(gate)
    act_low = (gate * sigmoid_gate * up_part).astype(jnp.bfloat16)
    mlp_out, down_full = keep_columns(
        act_low, lax.all_gather(down_weight, "dp", axis=0, tiled=True)
    )
    layer_out = hidden_res + mlp_out
    grad_low = cotangent.astype(jnp.bfloat16)
    grad_act = jnp.dot(grad_low, down_full, preferred_element_type=jnp.float32)
    grad_gate = grad_act * up_part * sigmoid_gate * (1.0 + gate * (1.0 - sigmoid_gate))
    grad_up = grad_act * gate * sigmoid_gate
    grad_gate_up = jnp.concatenate([grad_gate, grad_up], 1).astype(jnp.bfloat16)
    grad_xn2 = jnp.einsum(
        "tc,rc->tr", grad_gate_up, gate_up_full, preferred_element_type=jnp.float32
    )
    norm2_term = jnp.sum(grad_xn2 * normed2, axis=0)
    grad_hidden = cotangent + norm_backward(grad_xn2, normed2, norm2_gain, inv_rms2)
    hidden_low = grad_hidden.astype(jnp.bfloat16)
    grad_attn = jnp.einsum(
        "tc,rc->tr", hidden_low, out_full, preferred_element_type=jnp.float32
    ).astype(jnp.bfloat16)
    grad_heads = heads_from_tokens(grad_attn.reshape(token_rows, 1, group_count, group_width))
    grad_mixed = grad_heads[:, 0]
    grad_query, grad_key, grad_value = attend_backward(
        query_rot, key_rot, value_heads, mixed, log_total, grad_mixed
    )
    grad_query = rotate(grad_query, cosine, -sine)
    grad_key = rotate(grad_key, cosine, -sine)
    grad_stack = jnp.stack([grad_query, grad_key, grad_value], 1).astype(jnp.bfloat16)
    token_grads = tokens_from_heads(grad_stack)
    grad_qkv = token_grads.reshape(token_rows, 3 * model_width)
    grad_xn1 = jnp.einsum("tc,rc->tr", grad_qkv, qkv_full, preferred_element_type=jnp.float32)
    norm1_term = jnp.sum(grad_xn1 * normed1, axis=0)
    input_grad = grad_hidden + norm_backward(grad_xn1, normed1, norm1_gain, inv_rms1)
    norm_grads = (
        lax.psum_scatter(norm1_term, ("dp", "seq"), scatter_dimension=0, tiled=True),
        lax.psum_scatter(norm2_term, ("dp", "seq"), scatter_dimension=0, tiled=True),
    )
    widths = (3 * model_width, model_width, 2 * hidden_units, hidden_units)
    gathered_rows = (
        lax.all_gather(
            seq_major(xn_first, dp_count, group_count, shard_rows), "dp", axis=0, tiled=True
        ),
        lax.all_gather(
            seq_major(attn_low, dp_count, group_count, shard_rows), "dp", axis=0, tiled=True
        ),
        lax.all_gather(
            seq_major(xn_second, dp_count, group_count, shard_rows), "dp", axis=0, tiled=True
        ),
        lax.all_gather(
            seq_major(grad_low, dp_count, group_count, shard_rows), "dp", axis=0, tiled=True
        ),
    )
    split_cols = (
        lax.all_to_all(grad_qkv, "dp", split_axis=1, concat_axis=0, tiled=True),
        lax.all_to_all(hidden_low, "dp", split_axis=1, concat_axis=0, tiled=True),
        lax.all_to_all(grad_gate_up, "dp", split_axis=1, concat_axis=0, tiled=True),
        lax.all_to_all(act_low, "dp", split_axis=1, concat_axis=0, tiled=True),
    )
    stripes = lax.psum_scatter(
        jnp.concatenate(
            [row_product(gathered_rows[which], split_cols[which]) for which in range(4)], 1
        ).astype(jnp.bfloat16),
        "seq",
        scatter_dimension=0,
        tiled=True,
    ).astype(jnp.float32)
    owned_rows = (
        lax.all_to_all(stripes.astype(jnp.bfloat16), "dp", split_axis=0, concat_axis=1, tiled=True)
        .astype(stripes.dtype)
        .reshape(shard_rows, dp_count, -1)
    )
    pieces = []
    offset = 0
    for column_width in widths:
        share_cols = column_width // dp_count
        pieces.append(
            owned_rows[:, :, offset : offset + share_cols].reshape(shard_rows, column_width)
        )
        offset = offset + share_cols
    return (
        layer_out,
        input_grad,
        norm_grads[0],
        pieces[0],
        pieces[1],
        norm_grads[1],
        pieces[2],
        pieces[3],
    )


def solution(mesh):
    in_specs = (
        P(("dp", "seq"), None),
        P(),
        P("dp", None),
        P("dp", None),
        P(),
        P("dp", None),
        P("dp", None),
        P(("dp", "seq"), None),
    )
    out_specs = (
        P(("dp", "seq"), None),
        P(("dp", "seq"), None),
        P(("dp", "seq")),
        P(("dp", "seq"), None),
        P(("dp", "seq"), None),
        P(("dp", "seq")),
        P(("dp", "seq"), None),
        P(("dp", "seq"), None),
    )
    return jax.shard_map(shards, mesh=mesh, in_specs=in_specs, out_specs=out_specs, check_vma=False)
```

profile of v0, /device:TPU:0, one launch (start us, length us, event | category | flops | bytes accessed | tf_op | source)
XLA Modules:
  0.0 2005.1 jit_solution(732256753957964172)
XLA Ops:
  11.0 229.2 %all-gather.9.cloned.1.call-done = bf16[2048,6144]{1,0:T(8,128)(2,1)} async-done(((bf16[512,6144]{1,0:T(8,128)(2,1)}), bf16[2048,6144]{1,0:T(8,128)(2,1)}) %all-gather.9.cloned.1.call-update) | async-done | bytes 25165840 | tf_op jit(solution)/shard_map/all_gather | solution.py:150
  240.2 11.6 convolution_convert_fusion.2
  253.7 4.9 all-to-all-start
  260.0 36.4 %all-to-all-done = bf16[128,3,8,256]{3,0,1,2:T(8,128)(2,1)} async-done(((bf16[128,3,8,256]{3,0,1,2:T(8,128)(2,1)}), bf16[128,3,8,256]{3,0,1,2:T(8,128)(2,1)}, u32[]{:S(2)}, u32[]{:S(2)}) %all-to-all-start) | async-done | bytes 1572896 | tf_op jit(solution)/shard_map/all_to_all | solution.py:119
  306.0 16.1 while.27
  341.1 12.1 all-to-all-done.1
  357.7 7.2 multiply_reduce_fusion.5
  366.7 541.4 %all-gather.13.cloned.1.call-done = bf16[2048,16384]{1,0:T(8,128)(2,1)} async-done(((bf16[512,16384]{1,0:T(8,128)(2,1)}), bf16[2048,16384]{1,0:T(8,128)(2,1)}) %all-gather.13.cloned.1.call-update) | async-done | bytes 67108880 | tf_op jit(solution)/shard_map/all_gather | solution.py:167
  908.1 34.6 %fusion.51 = f32[128,16384]{1,0:T(8,128)} fusion(bf16[128,2048]{1,0:T(8,128)(2,1)S(1)} %multiply_convert_fusion.4, bf16[2048,16384]{1,0:T(8,128)(2,1)} %all-gather.13.cloned.1.call-done), kind=kOutput, calls=%fused_computation.121 | convolution fusion | flops 8589934592 | bytes 76021760 | tf_op jit(solution)/shard_map/dot_general | solution.py:105
  942.7 264.2 %all-gather.15.cloned.1.call-done = bf16[2048,8192]{1,0:T(8,128)(2,1)} async-done(((bf16[512,8192]{1,0:T(8,128)(2,1)}), bf16[2048,8192]{1,0:T(8,128)(2,1)}) %all-gather.15.cloned.1.call-update) | async-done | bytes 33554448 | tf_op jit(solution)/shard_map/all_gather | solution.py:174
  1206.9 19.6 multiply_convert_fusion.2
  1226.5 30.7 %multiply_reduce_fusion = (f32[2048]{0:T(1024)}, f32[128]{0:T(128)S(1)}, f32[128,2048]{1,0:T(8,128)}) fusion(f32[128,2048]{1,0:T(8,128)S(1)} %copy-done.4, f32[128]{0:T(128)S(1)} %add_rsqrt_fusion, f32[2048]{0:T(1024)S(1)} %copy-done.24, bf16[2048,16384]{1,0:T(8,128)(2,1)} %all-gather.13.cloned.1.call-done, bf16[128,8192]{1,0:T(8,128)(2,1)} %get-tuple-element.206, ...), kind=kOutput, calls=%fused_computation.84 | convolution fusion | flops 8599894016 | bytes 73417728 | tf_op jit(solution)/shard_map/tc,rc->tr/dot_general | solution.py:182
  1260.1 6.3 convolution_convert_fusion.4
  1273.7 13.6 all-to-all-done.2
  1306.3 72.6 %while.28 = (s32[]{:T(128)}, f32[1024,4,64]{0,2,1:T(8,128)S(1)}, f32[1024,4,64]{0,2,1:T(8,128)}, f32[2,512,4,64]{1,0,3,2:T(2,128)}, s32[2]{0:T(128)S(1)}, /*inde...) while((s32[]{:T(128)}, f32[1024,4,64]{0,2,1:T(8,128)S(1)}, ...), condition=%wide.region_9.10_spmd.clone, body=%wide.region_8.9_spmd.clone.sunk | while | flops 1366819328 | bytes 107540888 | solution.py:93
  1314.5 7.1 multiply_convert_fusion.7
  1332.2 10.4 dynamic_update_slice.20
  1350.8 7.1 multiply_convert_fusion.7
  1368.5 10.4 dynamic_update_slice.20
  1402.4 43.3 %all-to-all-done.3 = bf16[1024,3,1,256]{3,1,2,0:T(4,128)(2,1)} async-done(((bf16[1024,3,1,256]{3,1,2,0:T(4,128)(2,1)}), bf16[1024,3,1,256]{3,1,2,0:T(4,128)(2,1)}, u32[]{:S(2)}, u32[]{:S(2)}) %all-to-all-start.3) | async-done | bytes 1572896 | tf_op jit(solution)/shard_map/all_to_all | solution.py:126
  1445.7 4.9 all-to-all-start.6
  1459.0 10.3 convert_bitcast_fusion.1
  1474.8 40.3 %all-to-all-done.6 = bf16[128,4,4096]{2,0,1:T(8,128)(2,1)} async-done(((bf16[128,4,4096]{2,0,1:T(8,128)(2,1)}), bf16[128,4,4096]{2,0,1:T(8,128)(2,1)}, u32[]{:S(2)}, u32[]{:S(2)}) %all-to-all-start.6) | async-done | bytes 4194336 | tf_op jit(solution)/shard_map/all_to_all | solution.py:226
  1519.8 14.9 convolution_convert_fusion
  1539.5 8.2 convolution_convert_fusion.1
  1547.7 8.6 copy.149
  1556.3 22.2 %pad_maximum_fusion = bf16[2048,8192]{1,0:T(8,128)(2,1)} fusion(bf16[2048,2048]{1,0:T(8,128)(2,1)} %convert_bitcast_fusion.1, bf16[2048,4096]{1,0:T(8,128)(2,1)} %convolution_convert_fusion, bf16[2048,512]{1,0:T(8,128)(2,1)S(1)} %copy.150, bf16[2048,1536]{1,0:T(8,128)(2,1)} %copy.149), kind=kLoop, calls=%fused_computation.43 | loop fusion | flops 134217728 | bytes 67108864 | tf_op jit(solution)/shard_map/concatenate | solution.py:230
  1578.6 323.2 %reduce-scatter.2.cloned.1.call-done = bf16[256,8192]{1,0:T(8,128)(2,1)} async-done(((bf16[2048,8192]{1,0:T(8,128)(2,1)}), bf16[256,8192]{1,0:T(8,128)(2,1)}) %reduce-scatter.2.cloned.1.call-update) | async-done | bytes 4194320 | tf_op jit(solution)/shard_map/reduce_scatter | solution.py:229
  1901.7 5.3 all-to-all-start.8
  1907.1 17.4 convolution_add_fusion
  1924.5 13.8 multiply_reduce_fusion.1
  1938.3 47.7 %all-reduce.2 = (f32[2048]{0:T(1024)S(1)}, f32[2048]{0:T(1024)S(1)}) all-reduce(f32[2048]{0:T(1024)S(1)} %get-tuple-element.159, f32[2048]{0:T(1024)S(1)} %copy-done.25), channel_id=2, replica_groups=mesh['dp'=4,'seq'=8] {'dp','seq'}, use_global_device_ids=true, to_apply=%region_12.13.clone | all-reduce | flops 4096 | bytes 32768
  (216 shorter events, 176.4 us)
Async XLA Ops:
  7.2 233.0 %all-gather.9.cloned.1.call-start = ((), (), s32[]{:S(2)}) async-start(), calls=%async_computation.10 | async-start | bytes 31457280 | tf_op jit(solution)/shard_map/all_gather | solution.py:150
  7.9 349.8 %all-gather.11.cloned.1.call-start = ((), (), s32[]{:S(2)}) async-start(), calls=%async_computation.11 | async-start | bytes 10485760 | tf_op jit(solution)/shard_map/all_gather | solution.py:161
  8.6 899.4 %all-gather.13.cloned.1.call-start = ((), (), s32[]{:S(2)}) async-start(), calls=%async_computation.12 | async-start | bytes 83886080 | tf_op jit(solution)/shard_map/all_gather | solution.py:167
  9.4 1197.5 %all-gather.15.cloned.1.call-start = ((), (), s32[]{:S(2)}) async-start(), calls=%async_computation.13 | async-start | bytes 41943040 | tf_op jit(solution)/shard_map/all_gather | solution.py:174
  10.8 241.0 %copy-start.26 = (f32[128]{0:T(128)}, f32[128]{0:T(128)S(1)}, u32[]{:S(2)}) copy-start(f32[128]{0:T(128)S(1)} %add_rsqrt_fusion.1) | copy-start | bytes 1540
  11.0 240.8 %copy-start.9 = (bf16[128,2048]{1,0:T(8,128)(2,1)}, bf16[128,2048]{1,0:T(8,128)(2,1)S(1)}, u32[]{:S(2)}) copy-start(bf16[128,2048]{1,0:T(8,128)(2,1)S(1)} %multiply_convert_fusion.5) | copy-start | bytes 1572868
  253.7 42.7 %all-to-all-start = ((bf16[128,3,8,256]{3,0,1,2:T(8,128)(2,1)}), bf16[128,3,8,256]{3,0,1,2:T(8,128)(2,1)}, u32[]{:S(2)}, u32[]{:S(2)}) async-start(bf16[128,3,8,256]{3,0,1,2:T(8,128)(2,1)} %copy.121), calls=%async_computation | async-start | bytes 3145728 | tf_op jit(solution)/shard_map/all_to_all | solution.py:119
  259.2 46.4 %copy-start.11 = (f32[1024,64]{0,1:T(8,128)}, f32[1024,64]{0,1:T(8,128)S(1)}, u32[]{:S(2)}) copy-start(f32[1024,64]{0,1:T(8,128)S(1)} %pad_maximum_fusion.4) | copy-start | bytes 786436
  322.1 19.0 copy-start.16
  334.5 18.8 all-to-all-start.1
  338.0 1113.8 %all-gather.19.cloned.1.call-start = ((), (), s32[]{:S(2)}) async-start(), calls=%async_computation.15 | async-start | bytes 2621440 | tf_op jit(solution)/shard_map/all_gather | solution.py:213
  357.7 7.3 copy-start.24
  366.7 840.2 %copy-start.17 = (bf16[128,2048]{0,1:T(8,128)(2,1)S(1)}, bf16[128,2048]{0,1:T(8,128)(2,1)}, u32[]{:S(2)}) copy-start(bf16[128,2048]{0,1:T(8,128)(2,1)} %copy.126) | copy-start | bytes 1572868
  942.7 283.8 %copy-start.4 = (f32[128,2048]{1,0:T(8,128)S(1)}, f32[128,2048]{1,0:T(8,128)}, u32[]{:S(2)}) copy-start(f32[128,2048]{1,0:T(8,128)} %get-tuple-element.226) | copy-start | bytes 3145732
  1260.1 11.9 copy-start.18
  1267.4 19.9 all-to-all-start.2
  1271.9 187.1 %all-gather.23.cloned.1.call-start = ((), (), s32[]{:S(2)}) async-start(), calls=%async_computation.17 | async-start | bytes 2621440 | tf_op jit(solution)/shard_map/all_gather | solution.py:219
  1287.4 14.3 all-to-all-start.5
  1301.7 90.6 %all-to-all-start.7 = ((bf16[128,4,2048]{2,0,1:T(8,128)(2,1)}), bf16[128,4,2048]{2,0,1:T(8,128)(2,1)}, u32[]{:S(2)}, u32[]{:S(2)}) async-start(bf16[128,4,2048]{2,0,1:T(8,128)(2,1)} %bitcast.225), calls=%async_computation.7 | async-start | bytes 4194304 | tf_op jit(solution)/shard_map/all_to_all | solution.py:227
  1392.3 53.4 %all-to-all-start.3 = ((bf16[1024,3,1,256]{3,1,2,0:T(4,128)(2,1)}), bf16[1024,3,1,256]{3,1,2,0:T(4,128)(2,1)}, u32[]{:S(2)}, u32[]{:S(2)}) async-start(bf16[1024,3,1,256]{3,1,2,0:T(4,128)(2,1)} %copy.132), calls=%async_computation.3 | async-start | bytes 4194304 | tf_op jit(solution)/shard_map/all_to_all | solution.py:126
  1396.7 123.1 %all-gather.21.cloned.1.call-start = ((), (), s32[]{:S(2)}) async-start(), calls=%async_computation.16 | async-start | bytes 2621440 | tf_op jit(solution)/shard_map/all_gather | solution.py:216
  1402.4 48.2 %copy-start.10 = (bf16[128,2048]{1,0:T(8,128)(2,1)S(1)}, bf16[128,2048]{1,0:T(8,128)(2,1)}, u32[]{:S(2)}) copy-start(bf16[128,2048]{1,0:T(8,128)(2,1)} %copy-done.9) | copy-start | bytes 1572868
  1445.7 69.4 %all-to-all-start.6 = ((bf16[128,4,4096]{2,0,1:T(8,128)(2,1)}), bf16[128,4,4096]{2,0,1:T(8,128)(2,1)}, u32[]{:S(2)}, u32[]{:S(2)}) async-start(bf16[128,4,4096]{2,0,1:T(8,128)(2,1)} %pad_maximum_fusion.1), calls=%async_computation.6 | async-start | bytes 8388608 | tf_op jit(solution)/shard_map/all_to_all | solution.py:226
  1450.6 89.0 %all-gather.17.cloned.1.call-start = ((), (), s32[]{:S(2)}) async-start(), calls=%async_computation.14 | async-start | bytes 2621440 | tf_op jit(solution)/shard_map/all_gather | solution.py:210
  1515.1 21.9 %all-to-all-start.4 = ((bf16[128,4,1536]{0,2,1:T(8,128)(2,1)}), bf16[128,4,1536]{0,2,1:T(8,128)(2,1)}, u32[]{:S(2)}, u32[]{:S(2)}) async-start(bf16[128,4,1536]{0,2,1:T(8,128)(2,1)} %bitcast.30), calls=%async_computation.4 | async-start | bytes 3145728 | tf_op jit(solution)/shard_map/all_to_all | solution.py:224
  1519.4 382.3 %reduce-scatter.2.cloned.1.call-start = ((), (), s32[]{:S(2)}) async-start(), calls=%async_computation.18 | async-start | bytes 37748736 | tf_op jit(solution)/shard_map/reduce_scatter | solution.py:229
  1901.7 86.7 %all-to-all-start.8 = ((bf16[4,64,8192]{2,1,0:T(8,128)(2,1)}), bf16[4,64,8192]{2,1,0:T(8,128)(2,1)}, u32[]{:S(2)}, u32[]{:S(2)}) async-start(bf16[4,64,8192]{2,1,0:T(8,128)(2,1)} %bitcast.234), calls=%async_computation.9 | async-start | bytes 8388608 | tf_op jit(solution)/shard_map/all_to_all | solution.py:238
  1907.0 17.5 copy-start.3
  1907.0 17.5 copy-start.23
  1907.0 17.5 copy-start.27
  1924.5 13.8 copy-start.25
  1924.5 62.6 %copy-start.13 = (f32[128,2048]{1,0:T(8,128)S(1)}, f32[128,2048]{1,0:T(8,128)}, u32[]{:S(2)}) copy-start(f32[128,2048]{1,0:T(8,128)} %get-tuple-element.202) | copy-start | bytes 3145732
  (19 other events, 57.2 us)
Sparse Core Ops, SparseCore 0:
  9.8 230.2 all-gather.8
  242.0 87.4 all-gather.10
  331.4 576.6 all-gather.12
  909.8 297.0 all-gather.14
  1208.6 35.0 all-gather.18
  1274.2 51.1 all-gather.22
  1399.9 36.8 all-gather.20
  1453.8 61.1 all-gather.16
  1578.7 323.0 reduce-scatter.1
where the time goes:
time: 2010 us
  waiting for transfers between devices  1510 us (75%)
  matrix products  227 us (11%)
  local copies, waits for them, and re-layouts  99.7 us (5%)
  other arithmetic  55.9 us (3%)
  blocking collectives  47.7 us (2%)
  starting transfers between devices  41.8 us (2%)
    all_gather x1, waiting for transfers between devices, shards(): lax.all_gather(gate_up_weight, 'dp', axis=0, tiled=True)  541 us
    reduce_scatter x1, waiting for transfers between devices, shards(): lax.psum_scatter(jnp.concatenate([row_product(gathered_rows[which], split...  323 us
    all_gather x1, waiting for transfers between devices, shards(): lax.all_gather(down_weight, 'dp', axis=0, tiled=True)  264 us
    all_gather x1, waiting for transfers between devices, shards(): lax.all_gather(qkv_weight, 'dp', axis=0, tiled=True)  229 us
    all_to_all x2, waiting for transfers between devices, tokens_from_heads(): lax.all_to_all(flattened, 'seq', split_axis=0, concat_axis=2, tiled=True)  55.4 us
    dot_general x3, matrix products, keep_step(): running = jnp.dot(source, weight_piece, preferred_element_type=jnp.float32)  53.4 us
    all_to_all x2, waiting for transfers between devices, heads_from_tokens(): lax.all_to_all(token_block, 'seq', split_axis=2, concat_axis=0, tiled=True)  50.1 us
    unnamed x1, blocking collectives  47.7 us
  transfers between devices with their start and end apart: 18, of which 11 were waited for; matrix products, arithmetic and copies ran while one was open for 16% of the time, Pallas kernels for 0%

commit v1 on v0

--- a/solution.py
+++ b/solution.py
@@ -6,6 +6,11 @@
 HD = 64
 EPS = 1e-05
 THETA = 130000.0
+
+
+def all_by_exchange(x, mesh_axis, d):
+    sent = jnp.stack([x] * lax.axis_size(mesh_axis))
+    return jnp.concatenate(lax.all_to_all(sent, mesh_axis, 0, 0), axis=d)
 
 
 def rotary_tables(length, head_dim):
@@ -170,9 +175,7 @@
     up_part = gate_up[:, hidden_units:]
     sigmoid_gate = jax.nn.sigmoid(gate)
     act_low = (gate * sigmoid_gate * up_part).astype(jnp.bfloat16)
-    mlp_out, down_full = keep_columns(
-        act_low, lax.all_gather(down_weight, "dp", axis=0, tiled=True)
-    )
+    mlp_out, down_full = keep_columns(act_low, all_by_exchange(down_weight, "dp", 0))
     layer_out = hidden_res + mlp_out
     grad_low = cotangent.astype(jnp.bfloat16)
     grad_act = jnp.dot(grad_low, down_full, preferred_element_type=jnp.float32)

time: 2010 us -> 2090 us (1.040)
  waiting for transfers between devices: 1510 us -> 1560 us
  local copies, waits for them, and re-layouts: 99.7 us -> 121 us
    all_gather x1, waiting for transfers between devices: 541 us -> 865 us  [shards(): lax.all_gather(gate_up_weight, 'dp', axis=0, tiled=True)]
    all_gather x1 -> x0, waiting for transfers between devices: 264 us -> none  [shards(): lax.all_gather(down_weight, 'dp', axis=0, tiled=True)]
    all_to_all x2 -> x1, waiting for transfers between devices: 55.4 us -> 43.5 us  [tokens_from_heads(): lax.all_to_all(flattened, 'seq', split_axis=0, concat_axis=2, tiled=True)]
  transfers between devices with their start and end apart: 18 -> 17, of which waited for: 11 -> 9; matrix products, arithmetic and copies ran while one was open for 16% -> 16% of each run, Pallas kernels for 0% -> 0%
where the time goes in v1:
time: 2090 us
  waiting for transfers between devices  1560 us (75%)
  matrix products  218 us (10%)
  local copies, waits for them, and re-layouts  121 us (6%)
  blocking collectives  65.3 us (3%)
  other arithmetic  51.6 us (2%)
  starting transfers between devices  48.1 us (2%)
    all_gather x1, waiting for transfers between devices, shards(): lax.all_gather(gate_up_weight, 'dp', axis=0, tiled=True)  865 us
    reduce_scatter x1, waiting for transfers between devices, shards(): lax.psum_scatter(jnp.concatenate([row_product(gathered_rows[which], split...  323 us
    all_gather x1, waiting for transfers between devices, shards(): lax.all_gather(qkv_weight, 'dp', axis=0, tiled=True)  229 us
    all_to_all x2, waiting for transfers between devices, heads_from_tokens(): lax.all_to_all(token_block, 'seq', split_axis=2, concat_axis=0, tiled=True)  49.9 us
    unnamed x1, blocking collectives  47.6 us
    all_to_all x1, waiting for transfers between devices, tokens_from_heads(): lax.all_to_all(flattened, 'seq', split_axis=0, concat_axis=2, tiled=True)  43.5 us
    dot_general x3, matrix products, keep_step(): running = jnp.dot(source, weight_piece, preferred_element_type=jnp.float32)  42.9 us
  transfers between devices with their start and end apart: 17, of which 9 were waited for; matrix products, arithmetic and copies ran while one was open for 16% of the time, Pallas kernels for 0%

profile of v1, /device:TPU:0, one launch (start us, length us, event | category | flops | bytes accessed | tf_op | source)
XLA Modules:
  0.0 2085.2 jit_solution(8217282412140589770)
XLA Ops:
  10.7 229.4 %all-gather.8.cloned.1.call-done = bf16[2048,6144]{1,0:T(8,128)(2,1)} async-done(((bf16[512,6144]{1,0:T(8,128)(2,1)}), bf16[2048,6144]{1,0:T(8,128)(2,1)}) %all-gather.8.cloned.1.call-update) | async-done | bytes 25165840 | tf_op jit(solution)/shard_map/all_gather | solution.py:155
  240.2 11.6 convolution_convert_fusion.2
  260.0 36.3 %all-to-all-done = bf16[128,3,8,256]{3,0,1,2:T(8,128)(2,1)S(1)} async-done(((bf16[128,3,8,256]{3,0,1,2:T(8,128)(2,1)}), bf16[128,3,8,256]{3,0,1,2:T(8,128)(2,1)S(1)}, u32[]{:S(2)}, u32[]{:S(2)}) %all-to-all-start) | async-done | bytes 1572896 | tf_op jit(solution)/shard_map/all_to_all | solution.py:124
  303.8 17.7 while.27
  333.9 17.7 all_to_all.151
  351.7 19.7 stack.19
  371.3 9.8 all-to-all-start.2
  395.3 864.8 %all-gather.12.cloned.1.call-done = bf16[2048,16384]{1,0:T(8,128)(2,1)} async-done(((bf16[512,16384]{1,0:T(8,128)(2,1)}), bf16[2048,16384]{1,0:T(8,128)(2,1)}) %all-gather.12.cloned.1.call-update) | async-done | bytes 67108880 | tf_op jit(solution)/shard_map/all_gather | solution.py:172
  1260.1 26.6 %fusion.51 = f32[128,16384]{1,0:T(8,128)} fusion(bf16[128,2048]{1,0:T(8,128)(2,1)S(1)} %multiply_convert_fusion.4, bf16[2048,16384]{1,0:T(8,128)(2,1)} %all-gather.12.cloned.1.call-done), kind=kOutput, calls=%fused_computation.121 | convolution fusion | flops 8589934592 | bytes 76021760 | tf_op jit(solution)/shard_map/dot_general | solution.py:110
  1286.7 19.2 multiply_convert_fusion.2
  1305.8 30.5 %multiply_reduce_fusion = (f32[2048]{0:T(1024)}, f32[128]{0:T(128)S(1)}, f32[128,2048]{1,0:T(8,128)}) fusion(f32[128,2048]{1,0:T(8,128)S(1)} %copy-done.4, f32[128]{0:T(128)S(1)} %add_rsqrt_fusion, f32[2048]{0:T(1024)S(1)} %copy-done.29, bf16[2048,16384]{1,0:T(8,128)(2,1)} %all-gather.12.cloned.1.call-done, bf16[128,8192]{1,0:T(8,128)(2,1)} %get-tuple-element.206, ...), kind=kOutput, calls=%fused_computation.84 | convolution fusion | flops 8599894016 | bytes 73417728 | tf_op jit(solution)/shard_map/tc,rc->tr/dot_general | solution.py:185
  1339.2 6.3 convolution_convert_fusion.4
  1353.0 13.6 all-to-all-done.3
  1385.5 75.2 %while.28 = (s32[]{:T(128)}, f32[1024,4,64]{0,2,1:T(8,128)S(1)}, f32[1024,4,64]{0,2,1:T(8,128)}, f32[2,512,4,64]{1,0,3,2:T(2,128)}, s32[2]{0:T(128)S(1)}, /*inde...) while((s32[]{:T(128)}, f32[1024,4,64]{0,2,1:T(8,128)S(1)}, ...), condition=%wide.region_9.10_spmd.clone, body=%wide.region_8.9_spmd.clone.sunk | while | flops 1366819328 | bytes 69792104 | solution.py:98
  1393.8 5.8 multiply_convert_fusion.7
  1403.6 10.4 dynamic_update_slice.20
  1417.2 5.8 fusion.115
  1431.2 5.8 multiply_convert_fusion.7
  1441.0 10.4 dynamic_update_slice.20
  1454.6 6.1 fusion.115
  1481.9 43.5 %all-to-all-done.4 = bf16[1024,3,1,256]{3,1,2,0:T(4,128)(2,1)} async-done(((bf16[1024,3,1,256]{3,1,2,0:T(4,128)(2,1)}), bf16[1024,3,1,256]{3,1,2,0:T(4,128)(2,1)}, u32[]{:S(2)}, u32[]{:S(2)}) %all-to-all-start.4) | async-done | bytes 1572896 | tf_op jit(solution)/shard_map/all_to_all | solution.py:131
  1538.9 10.3 convert_bitcast_fusion.1
  1554.7 40.2 %all-to-all-done.7 = bf16[128,4,4096]{2,0,1:T(8,128)(2,1)} async-done(((bf16[128,4,4096]{2,0,1:T(8,128)(2,1)}), bf16[128,4,4096]{2,0,1:T(8,128)(2,1)}, u32[]{:S(2)}, u32[]{:S(2)}) %all-to-all-start.7) | async-done | bytes 4194336 | tf_op jit(solution)/shard_map/all_to_all | solution.py:229
  1599.6 14.9 convolution_convert_fusion
  1619.3 8.2 convolution_convert_fusion.1
  1627.5 8.7 copy.149
  1636.1 22.2 %pad_maximum_fusion = bf16[2048,8192]{1,0:T(8,128)(2,1)} fusion(bf16[2048,2048]{1,0:T(8,128)(2,1)} %convert_bitcast_fusion.1, bf16[2048,4096]{1,0:T(8,128)(2,1)} %convolution_convert_fusion, bf16[2048,512]{1,0:T(8,128)(2,1)S(1)} %copy.150, bf16[2048,1536]{1,0:T(8,128)(2,1)} %copy.149), kind=kLoop, calls=%fused_computation.43 | loop fusion | flops 134217728 | bytes 67108864 | tf_op jit(solution)/shard_map/concatenate | solution.py:233
  1658.4 323.2 %reduce-scatter.2.cloned.1.call-done = bf16[256,8192]{1,0:T(8,128)(2,1)} async-done(((bf16[2048,8192]{1,0:T(8,128)(2,1)}), bf16[256,8192]{1,0:T(8,128)(2,1)}) %reduce-scatter.2.cloned.1.call-update) | async-done | bytes 4194320 | tf_op jit(solution)/shard_map/reduce_scatter | solution.py:232
  1981.6 5.3 all-to-all-start.9
  1986.9 17.4 convolution_add_fusion
  2004.4 13.8 multiply_reduce_fusion.1
  2018.2 47.6 %all-reduce.2 = (f32[2048]{0:T(1024)S(1)}, f32[2048]{0:T(1024)S(1)}) all-reduce(f32[2048]{0:T(1024)S(1)} %get-tuple-element.159, f32[2048]{0:T(1024)S(1)} %copy-done.30), channel_id=2, replica_groups=mesh['dp'=4,'seq'=8] {'dp','seq'}, use_global_device_ids=true, to_apply=%region_12.13.clone | all-reduce | flops 4096 | bytes 32768
  (227 shorter events, 178.0 us)
Async XLA Ops:
  7.2 233.0 %all-gather.8.cloned.1.call-start = ((), (), s32[]{:S(2)}) async-start(), calls=%async_computation.11 | async-start | bytes 31457280 | tf_op jit(solution)/shard_map/all_gather | solution.py:155
  7.9 381.4 %all-gather.10.cloned.1.call-start = ((), (), s32[]{:S(2)}) async-start(), calls=%async_computation.12 | async-start | bytes 10485760 | tf_op jit(solution)/shard_map/all_gather | solution.py:166
  8.7 1251.4 %all-gather.12.cloned.1.call-start = ((), (), s32[]{:S(2)}) async-start(), calls=%async_computation.13 | async-start | bytes 83886080 | tf_op jit(solution)/shard_map/all_gather | solution.py:172
  10.7 241.0 %copy-start.9 = (bf16[128,2048]{1,0:T(8,128)(2,1)}, bf16[128,2048]{1,0:T(8,128)(2,1)S(1)}, u32[]{:S(2)}) copy-start(bf16[128,2048]{1,0:T(8,128)(2,1)S(1)} %multiply_convert_fusion.5) | copy-start | bytes 1572868
  253.7 42.6 %all-to-all-start = ((bf16[128,3,8,256]{3,0,1,2:T(8,128)(2,1)}), bf16[128,3,8,256]{3,0,1,2:T(8,128)(2,1)S(1)}, u32[]{:S(2)}, u32[]{:S(2)}) async-start(bf16[128,3,8,256]{3,0,1,2:T(8,128)(2,1)} %copy.121), calls=%async_computation | async-start | bytes 3145728 | tf_op jit(solution)/shard_map/all_to_all | solution.py:124
  259.1 43.0 %copy-start.13 = (f32[1024,64]{0,1:T(8,128)}, f32[1024,64]{0,1:T(8,128)S(1)}, u32[]{:S(2)}) copy-start(f32[1024,64]{0,1:T(8,128)S(1)} %pad_maximum_fusion.4) | copy-start | bytes 786436
  371.3 915.3 %all-to-all-start.2 = ((bf16[4,512,8192]{2,1,0:T(8,128)(2,1)}), bf16[4,512,8192]{2,1,0:T(8,128)(2,1)}, u32[]{:S(2)}, u32[]{:S(2)}) async-start(bf16[4,512,8192]{2,1,0:T(8,128)(2,1)} %stack.19), calls=%async_computation.2 | async-start | bytes 67108864 | tf_op jit(solution)/shard_map/all_to_all | solution.py:13
  381.2 1150.5 %all-gather.16.cloned.1.call-start = ((), (), s32[]{:S(2)}) async-start(), calls=%async_computation.15 | async-start | bytes 2621440 | tf_op jit(solution)/shard_map/all_gather | solution.py:216
  383.2 903.5 %copy-start.23 = (bf16[128,2048]{0,1:T(8,128)(2,1)}, bf16[128,2048]{0,1:T(8,128)(2,1)S(1)}, u32[]{:S(2)}) copy-start(bf16[128,2048]{0,1:T(8,128)(2,1)S(1)} %copy.126) | copy-start | bytes 1572868
  395.2 891.4 %copy-start.11 = (bf16[128,2048]{1,0:T(8,128)(2,1)}, bf16[128,2048]{1,0:T(8,128)(2,1)S(1)}, u32[]{:S(2)}) copy-start(bf16[128,2048]{1,0:T(8,128)(2,1)S(1)} %multiply_convert_fusion.4) | copy-start | bytes 1572868
  1286.6 19.2 copy-start.4
  1339.2 12.0 copy-start.24
  1345.5 25.2 %copy-start.20 = (bf16[2,512,4,64]{1,3,2,0:T(8,128)(2,1)S(1)}, bf16[2,512,4,64]{1,3,2,0:T(8,128)(2,1)}, u32[]{:S(2)}) copy-start(bf16[2,512,4,64]{1,3,2,0:T(8,128)(2,1)} %get-tuple-element.105) | copy-start | bytes 1572868
  1346.6 20.0 all-to-all-start.3
  1351.1 187.7 %all-gather.20.cloned.1.call-start = ((), (), s32[]{:S(2)}) async-start(), calls=%async_computation.17 | async-start | bytes 2621440 | tf_op jit(solution)/shard_map/all_gather | solution.py:222
  1366.6 14.3 all-to-all-start.6
  1380.9 91.1 %all-to-all-start.8 = ((bf16[128,4,2048]{2,0,1:T(8,128)(2,1)}), bf16[128,4,2048]{2,0,1:T(8,128)(2,1)}, u32[]{:S(2)}, u32[]{:S(2)}) async-start(bf16[128,4,2048]{2,0,1:T(8,128)(2,1)} %bitcast.226), calls=%async_computation.8 | async-start | bytes 4194304 | tf_op jit(solution)/shard_map/all_to_all | solution.py:230
  1385.5 8.3 copy-start.21
  1423.0 8.3 copy-start.21
  1472.0 53.4 %all-to-all-start.4 = ((bf16[1024,3,1,256]{3,1,2,0:T(4,128)(2,1)}), bf16[1024,3,1,256]{3,1,2,0:T(4,128)(2,1)}, u32[]{:S(2)}, u32[]{:S(2)}) async-start(bf16[1024,3,1,256]{3,1,2,0:T(4,128)(2,1)} %copy.132), calls=%async_computation.4 | async-start | bytes 4194304 | tf_op jit(solution)/shard_map/all_to_all | solution.py:131
  1476.3 123.2 %all-gather.18.cloned.1.call-start = ((), (), s32[]{:S(2)}) async-start(), calls=%async_computation.16 | async-start | bytes 2621440 | tf_op jit(solution)/shard_map/all_gather | solution.py:219
  1481.9 48.6 %copy-start.10 = (bf16[128,2048]{1,0:T(8,128)(2,1)S(1)}, bf16[128,2048]{1,0:T(8,128)(2,1)}, u32[]{:S(2)}) copy-start(bf16[128,2048]{1,0:T(8,128)(2,1)} %copy-done.9) | copy-start | bytes 1572868
  1525.3 69.6 %all-to-all-start.7 = ((bf16[128,4,4096]{2,0,1:T(8,128)(2,1)}), bf16[128,4,4096]{2,0,1:T(8,128)(2,1)}, u32[]{:S(2)}, u32[]{:S(2)}) async-start(bf16[128,4,4096]{2,0,1:T(8,128)(2,1)} %pad_maximum_fusion.1), calls=%async_computation.7 | async-start | bytes 8388608 | tf_op jit(solution)/shard_map/all_to_all | solution.py:229
  1530.4 88.8 %all-gather.14.cloned.1.call-start = ((), (), s32[]{:S(2)}) async-start(), calls=%async_computation.14 | async-start | bytes 2621440 | tf_op jit(solution)/shard_map/all_gather | solution.py:213
  1594.9 21.8 %all-to-all-start.5 = ((bf16[128,4,1536]{0,2,1:T(8,128)(2,1)}), bf16[128,4,1536]{0,2,1:T(8,128)(2,1)}, u32[]{:S(2)}, u32[]{:S(2)}) async-start(bf16[128,4,1536]{0,2,1:T(8,128)(2,1)} %bitcast.31), calls=%async_computation.5 | async-start | bytes 3145728 | tf_op jit(solution)/shard_map/all_to_all | solution.py:227
  1599.2 382.3 %reduce-scatter.2.cloned.1.call-start = ((), (), s32[]{:S(2)}) async-start(), calls=%async_computation.18 | async-start | bytes 37748736 | tf_op jit(solution)/shard_map/reduce_scatter | solution.py:232
  1981.6 86.7 %all-to-all-start.9 = ((bf16[4,64,8192]{2,1,0:T(8,128)(2,1)}), bf16[4,64,8192]{2,1,0:T(8,128)(2,1)}, u32[]{:S(2)}, u32[]{:S(2)}) async-start(bf16[4,64,8192]{2,1,0:T(8,128)(2,1)} %bitcast.236), calls=%async_computation.10 | async-start | bytes 8388608 | tf_op jit(solution)/shard_map/all_to_all | solution.py:241
  1986.9 17.5 copy-start.2
  1986.9 17.5 copy-start.28
  1986.9 17.5 copy-start.32
  2004.3 13.8 copy-start.30
  2004.4 62.6 %copy-start.15 = (f32[128,2048]{1,0:T(8,128)S(1)}, f32[128,2048]{1,0:T(8,128)}, u32[]{:S(2)}) copy-start(f32[128,2048]{1,0:T(8,128)} %get-tuple-element.202) | copy-start | bytes 3145732
  (24 other events, 56.4 us)
Sparse Core Ops, SparseCore 0:
  9.8 230.2 all-gather.7
  242.0 87.4 all-gather.9
  331.4 928.6 all-gather.11
  1261.7 35.0 all-gather.15
  1353.5 51.6 all-gather.19
  1479.2 36.8 all-gather.17
  1533.7 61.1 all-gather.13
  1658.5 323.0 reduce-scatter.1
